TPU v7x, 128 devices: a whole 4x4x4 slice. The times are simulated.
128 devices in a mesh: dp: 8 (over y, core), tensor: 16 (over z, x).
Axes of the slice: x: 4, y: 4, z: 4, core: 2. Of those that a mesh axis runs over, the one named last changes fastest.
Arguments:
- thinker_rows: bfloat16 [16384, 8192], P('dp', 'tensor'), may hold values from -6 to 6
- proj_weight: bfloat16 [8192, 3584], P('tensor'), may hold values from -0.0625 to 0.0625
- proj_bias: float32 [3584], replicated, may hold values from -3 to 3
- cotangent: bfloat16 [16384, 3584], P('dp'), may hold values from -6 to 6
- block_owner: int32 [128], P('dp'), may hold values from 0 to 7, as said below
- block_offset: int32 [128], P('dp'), may hold values from 0 to 31, as said below
Outputs:
- grad_thinker: bfloat16 [32768, 8192], P('dp', 'tensor')
- proj_grad: float32 [8192, 3584], P(('tensor', 'dp'))
Inputs may be any that keep to these rules, and one draw needn't show every extreme that they name: `block_owner`: the 16 blocks of one index of dp name at most 4 blocks for any one owner, and the blocks for one owner stand next to each other; one owner receives exactly 4 blocks from every index of dp. `block_offset`: no two talker blocks share both owner and offset.
All inputs are finite; a program needn't handle non-finite values.
Results may differ from a plain program's by a relative error of at most 0.015.
Values may be sent and summed in bfloat16 or wider, within the bound.
A program may use at most 128 MiB of HBM per device.

v0:
```python
import jax
import jax.numpy as jnp
from jax import lax
from jax.sharding import PartitionSpec as P

BLOCK = 128


def slope_of(summed, proj_bias, cot_rows):
    pre_act = summed + proj_bias
    gate_value = jax.nn.sigmoid(pre_act)
    return (
        cot_rows.astype(jnp.float32) * gate_value * (1.0 + pre_act * (1.0 - gate_value))
    ).astype(jnp.bfloat16)


def return_rows(input_grad, block_owner, block_offset, dp_count):
    row_count, local_width = input_grad.shape
    block_total = row_count // BLOCK
    slot_cap = 2 * block_total // dp_count
    slot_total = dp_count * slot_cap
    pieces = input_grad.reshape(block_total, BLOCK, local_width)
    owner_hot = (block_owner[:, None] == jnp.arange(dp_count, dtype=jnp.int32)[None, :]).astype(
        jnp.int32
    )
    within = jnp.sum((jnp.cumsum(owner_hot, axis=0) - owner_hot) * owner_hot, axis=1)
    slot_index = block_owner * slot_cap + within
    slot_match = slot_index[None, :] == jnp.arange(slot_total, dtype=jnp.int32)[:, None]
    filled = jnp.any(slot_match, axis=1)
    picked = jnp.sum(
        jnp.where(slot_match, jnp.arange(block_total, dtype=jnp.int32)[None, :], 0), axis=1
    )
    send_rows = jnp.where(filled[:, None, None], pieces[picked], jnp.zeros((), jnp.bfloat16))
    send_rows = send_rows.reshape(dp_count, slot_cap, BLOCK, local_width)
    send_offset = jnp.where(filled, block_offset[picked], -1).reshape(dp_count, slot_cap)
    got_rows, got_offset = (
        lax.all_to_all(send_rows, "dp", split_axis=0, concat_axis=0, tiled=True),
        lax.all_to_all(send_offset, "dp", split_axis=0, concat_axis=0, tiled=True),
    )
    chooser = (
        got_offset.reshape(slot_total)[None, :]
        == jnp.arange(2 * block_total, dtype=jnp.int32)[:, None]
    ).astype(jnp.bfloat16)
    owner_grad = jnp.dot(
        chooser,
        got_rows.reshape(slot_total, BLOCK * local_width),
        preferred_element_type=jnp.float32,
    )
    return owner_grad.astype(jnp.bfloat16).reshape(2 * block_total * BLOCK, local_width)


def shards(thinker_rows, proj_weight, proj_bias, cotangent, block_owner, block_offset):
    row_count, local_width = thinker_rows.shape
    tensor_count = lax.axis_size("tensor")
    dp_count = lax.axis_size("dp")
    share_rows = row_count // tensor_count
    summed = lax.psum_scatter(
        jnp.dot(thinker_rows, proj_weight, preferred_element_type=jnp.float32).astype(jnp.bfloat16),
        "tensor",
        scatter_dimension=0,
        tiled=True,
    ).astype(jnp.float32)
    own_cot = lax.dynamic_slice_in_dim(
        cotangent, lax.axis_index("tensor") * share_rows, share_rows, 0
    )
    slope_rows = lax.all_gather(slope_of(summed, proj_bias, own_cot), "tensor", axis=0, tiled=True)
    input_grad = lax.dot_general(
        slope_rows, proj_weight, (((1,), (1,)), ((), ())), preferred_element_type=jnp.float32
    ).astype(jnp.bfloat16)
    grad_scale = float(row_count * dp_count) ** (-0.5)
    weight_term = (
        lax.dot_general(
            thinker_rows, slope_rows, (((0,), (0,)), ((), ())), preferred_element_type=jnp.float32
        )
        * grad_scale
    )
    proj_grad = lax.psum_scatter(
        weight_term.astype(jnp.bfloat16), "dp", scatter_dimension=0, tiled=True
    ).astype(jnp.float32)
    grad_thinker = return_rows(input_grad, block_owner, block_offset, dp_count)
    return (grad_thinker, proj_grad)


def solution(mesh):
    return jax.shard_map(
        shards,
        mesh=mesh,
        in_specs=(P("dp", "tensor"), P("tensor", None), P(), P("dp", None), P("dp"), P("dp")),
        out_specs=(P("dp", "tensor"), P(("tensor", "dp"), None)),
        check_vma=False,
    )
```

profile of v0, /device:TPU:1, one launch (start us, length us, event | category | flops | bytes accessed | tf_op | source)
XLA Modules:
  0.0 352.0 jit_solution(12200362587579199191)
XLA Ops:
  7.2 0.0 copy-start
  7.2 0.0 reduce-scatter.5.cloned.1.call-start
  7.2 1.5 copy-done
  8.8 13.0 %convolution_convert_fusion.1 = bf16[2048,3584]{1,0:T(8,128)(2,1)} fusion(bf16[2048,512]{1,0:T(8,128)(2,1)S(1)} %copy-done, bf16[512,3584]{1,0:T(8,128)(2,1)} %param.7), kind=kOutput, calls=%fused_computation.3 | convolution fusion | flops 7523532800 | bytes 20447232 | tf_op jit(solution)/shard_map/dot_general | solution.py:58
  21.8 0.0 copy-start.3
  21.8 0.0 reduce-scatter.5.cloned.1.call-update
  21.8 0.0 copy-start.4
  21.8 0.0 all-gather.2.cloned.1.call-start
  21.9 105.5 %reduce-scatter.5.cloned.1.call-done = bf16[128,3584]{1,0:T(8,128)(2,1)} async-done(((bf16[2048,3584]{1,0:T(8,128)(2,1)}), bf16[128,3584]{1,0:T(8,128)(2,1)}) %reduce-scatter.5.cloned.1.call-update) | async-done | bytes 917520 | tf_op jit(solution)/shard_map/reduce_scatter | solution.py:57
  127.4 0.0 copy-done.3
  127.4 3.1 multiply_convert_fusion.1
  130.5 0.0 all-gather.2.cloned.1.call-update
  130.5 0.0 reduce-scatter.7.cloned.1.call-start
  130.6 0.0 copy-done.4
  130.6 0.1 fusion.3
  130.7 99.5 %all-gather.2.cloned.1.call-done = bf16[2048,3584]{1,0:T(8,128)(2,1)} async-done(((bf16[128,3584]{1,0:T(8,128)(2,1)}), bf16[2048,3584]{1,0:T(8,128)(2,1)}) %all-gather.2.cloned.1.call-update) | async-done | bytes 14680080 | tf_op jit(solution)/shard_map/all_gather | solution.py:66
  230.2 12.3 %fusion = bf16[512,3584]{0,1:T(8,128)(2,1)} fusion(bf16[2048,3584]{1,0:T(8,128)(2,1)} %all-gather.2.cloned.1.call-done, bf16[2048,512]{1,0:T(8,128)(2,1)S(1)} %copy-done), kind=kOutput, calls=%fused_computation.5 | convolution fusion | flops 7519862784 | bytes 20447232 | tf_op jit(solution)/shard_map/dot_general | solution.py:72
  242.6 5.9 %copy.14 = bf16[512,3584]{1,0:T(8,128)(2,1)} copy(bf16[512,3584]{0,1:T(8,128)(2,1)} %fusion) | data formatting | bytes 7340032
  248.4 0.0 copy-start.2
  248.4 0.0 reduce-scatter.7.cloned.1.call-update
  248.5 0.2 select_reduce_fusion.1
  248.6 0.1 select_reduce_fusion
  248.8 0.3 copy-done.2
  249.1 0.7 gather_fusion
  249.8 0.1 fusion.2
  249.9 0.7 select_n.41
  250.6 5.1 %all-to-all-start = ((s32[8,1,4]{2,1,0:T(1,128)}), s32[8,1,4]{2,1,0:T(1,128)S(1)}, u32[]{:S(2)}, u32[]{:S(2)}) async-start(s32[8,1,4]{2,1,0:T(1,128)} %bitcast.2), calls=%async_computation | async-start | bytes 8192 | tf_op jit(solution)/shard_map/all_to_all | solution.py:38
  255.7 0.1 broadcast_in_dim.43
  255.8 12.5 %convolution_convert_fusion.2 = bf16[2048,512]{1,0:T(8,128)(2,1)S(1)} fusion(bf16[2048,3584]{1,0:T(8,128)(2,1)} %all-gather.2.cloned.1.call-done, bf16[512,3584]{1,0:T(8,128)(2,1)} %param.7), kind=kOutput, calls=%fused_computation.7 | convolution fusion | flops 7517241344 | bytes 20447232 | tf_op jit(solution)/shard_map/dot_general | solution.py:67
  268.2 2.8 gather_fusion.1
  271.1 4.6 %broadcast_select_fusion = bf16[8,4,128,512]{3,2,1,0:T(8,128)(2,1)} fusion(bf16[8,4,128,512]{3,2,1,0:T(8,128)(2,1)} %bitcast.20, pred[8,4]{1,0:T(8,128)(4,1)S(1)} %broadcast_in_dim.43), kind=kLoop, calls=%fused_computation.6 | loop fusion | flops 2097152 | bytes 8388640 | tf_op jit(solution)/shard_map/jit(_where)/select_n | solution.py:33
  275.7 0.0 all-to-all-done
  275.7 4.8 %all-to-all-start.1 = ((bf16[8,4,128,512]{3,2,1,0:T(8,128)(2,1)}), bf16[8,4,128,512]{3,2,1,0:T(8,128)(2,1)}, u32[]{:S(2)}, u32[]{:S(2)}) async-start(bf16[8,4,128,512]{3,2,1,0:T(8,128)(2,1)} %broadcast_select_fusion), calls=%async_computation.2 | async-start | bytes 8388608 | tf_op jit(solution)/shard_map/all_to_all | solution.py:37
  280.5 0.5 broadcast.65
  281.0 0.7 reduce.3
  281.7 0.1 eq.47
  281.8 47.5 %all-to-all-done.1 = bf16[8,4,128,512]{3,2,1,0:T(8,128)(2,1)} async-done(((bf16[8,4,128,512]{3,2,1,0:T(8,128)(2,1)}), bf16[8,4,128,512]{3,2,1,0:T(8,128)(2,1)}, u32[]{:S(2)}, u32[]{:S(2)}) %all-to-all-start.1) | async-done | bytes 4194336 | tf_op jit(solution)/shard_map/all_to_all | solution.py:37
  329.3 4.6 %copy.16 = bf16[4,8,128,512]{3,1,2,0:T(8,128)(2,1)S(1)} copy(bf16[4,8,128,512]{3,2,1,0:T(8,128)(2,1)} %bitcast.8) | data formatting | bytes 8388608
  333.9 3.2 convolution_convert_fusion
  337.0 0.0 copy-start.1
  337.0 5.8 %reshape.62 = bf16[4096,512]{1,0:T(8,128)(2,1)} reshape(bf16[32,65536]{1,0:T(8,128)(2,1)} %convolution_convert_fusion) | data formatting | bytes 8388608 | tf_op jit(solution)/shard_map/reshape | solution.py:49
  342.8 0.0 reduce-scatter.7.cloned.1.call-done
  342.8 1.4 copy.15
  344.2 1.2 copy.13
  345.5 0.0 copy-done.1
  (5 shorter events, 0.1 us)
Async XLA Ops:
  7.2 1.6 copy-start
  7.2 120.2 %reduce-scatter.5.cloned.1.call-start = ((), (), s32[]{:S(2)}) async-start(), calls=%async_computation.4 | async-start | bytes 15597568 | tf_op jit(solution)/shard_map/reduce_scatter | solution.py:57
  21.8 105.6 %copy-start.3 = (f32[3584]{0:T(1024)S(1)}, f32[3584]{0:T(1024)}, u32[]{:S(2)}) copy-start(f32[3584]{0:T(1024)} %param.8) | copy-start | bytes 43012
  21.8 108.8 %copy-start.4 = (s32[16]{0:T(128)S(1)}, s32[16]{0:T(128)}, u32[]{:S(2)}) copy-start(s32[16]{0:T(128)} %param.10) | copy-start | bytes 196
  21.8 208.4 %all-gather.2.cloned.1.call-start = ((), (), s32[]{:S(2)}) async-start(), calls=%async_computation.5 | async-start | bytes 15597568 | tf_op jit(solution)/shard_map/all_gather | solution.py:66
  130.5 212.3 %reduce-scatter.7.cloned.1.call-start = ((), (), s32[]{:S(2)}) async-start(), calls=%async_computation.6 | async-start | bytes 4128768
  248.4 0.7 copy-start.2
  250.6 25.1 %all-to-all-start = ((s32[8,1,4]{2,1,0:T(1,128)}), s32[8,1,4]{2,1,0:T(1,128)S(1)}, u32[]{:S(2)}, u32[]{:S(2)}) async-start(s32[8,1,4]{2,1,0:T(1,128)} %bitcast.2), calls=%async_computation | async-start | bytes 8192 | tf_op jit(solution)/shard_map/all_to_all | solution.py:38
  275.7 53.6 %all-to-all-start.1 = ((bf16[8,4,128,512]{3,2,1,0:T(8,128)(2,1)}), bf16[8,4,128,512]{3,2,1,0:T(8,128)(2,1)}, u32[]{:S(2)}, u32[]{:S(2)}) async-start(bf16[8,4,128,512]{3,2,1,0:T(8,128)(2,1)} %broadcast_select_fusion), calls=%async_computation.2 | async-start | bytes 8388608 | tf_op jit(solution)/shard_map/all_to_all | solution.py:37
  337.0 8.5 %copy-start.1 = (bf16[2048,512]{1,0:T(8,128)(2,1)S(1)}, bf16[2048,512]{1,0:T(8,128)(2,1)}, u32[]{:S(2)}) copy-start(bf16[2048,512]{1,0:T(8,128)(2,1)} %param.6) | copy-start | bytes 6291460
Sparse Core Ops, SparseCore 0:
  21.9 105.3 reduce-scatter.4
  130.6 99.5 all-gather.1
  248.6 33.6 reduce-scatter.6
where the time goes:
time: 353 us; the launch traced here: 352 us
  waiting for transfers between devices  253 us (72%)
  matrix products  41 us (12%)
  local copies, waits for them, and re-layouts  25.6 us (7%)
  between operations  13.8 us (4%)
  starting transfers between devices  10.1 us (3%)
  other arithmetic  8.91 us (3%)
    reduce_scatter x1, waiting for transfers between devices, shards(): lax.psum_scatter(jnp.dot(thinker_rows, proj_weight, preferred_element_typ...  105 us
    all_gather x1, waiting for transfers between devices, shards(): lax.all_gather(slope_of(summed, proj_bias, own_cot), 'tensor', axis=0, ti...  99.5 us
    all_to_all x1, waiting for transfers between devices, return_rows(): lax.all_to_all(send_rows, 'dp', split_axis=0, concat_axis=0, tiled=True)  47.5 us
    unnamed x14, local copies, waits for them, and re-layouts  15 us
    dot_general x1, matrix products, shards(): jnp.dot(thinker_rows, proj_weight, preferred_element_type=jnp.float32)  13 us
    dot_general x1, matrix products, shards(): lax.dot_general(slope_rows, proj_weight, (((1,), (1,)), ((), ())), prefer...  12.5 us
    dot_general x1, matrix products, shards(): lax.dot_general(thinker_rows, slope_rows, (((0,), (0,)), ((), ())), prefe...  12.3 us
  transfers between devices with their start and end apart: 5, of which 3 were waited for; matrix products, arithmetic and copies ran while one was open for 10% of the time, Pallas kernels for 0%

commit v1 on v0

v1 whole, which is shorter than its diff:
```python
import jax
import jax.numpy as jnp
from jax import lax
from jax.experimental import pallas as pl
from jax.experimental.pallas import tpu as pltpu
from jax.sharding import PartitionSpec as P

BLOCK = 128
CHUNKS = 4


def slope_of(summed, proj_bias, cot_rows):
    pre_act = summed + proj_bias
    gate_value = jax.nn.sigmoid(pre_act)
    return (
        cot_rows.astype(jnp.float32) * gate_value * (1.0 + pre_act * (1.0 - gate_value))
    ).astype(jnp.bfloat16)


def place_kernel(pick, valid, *refs):
    got, (out, held, zeros, in_sem, out_sem) = refs[:CHUNKS], refs[CHUNKS:]
    count = out.shape[0]
    slots = count // CHUNKS
    loads = [
        pltpu.make_async_copy(got[c], held.at[pl.ds(c * slots, slots)], in_sem.at[c])
        for c in range(CHUNKS)
    ]
    for load in loads:
        load.start()
    zeros[...] = jnp.zeros_like(zeros)
    for load in loads:
        load.wait()
    for j in range(count):

        @pl.when(valid[j] != 0)
        def _():
            pltpu.make_async_copy(held.at[pick[j]], out.at[j], out_sem).start()

        @pl.when(valid[j] == 0)
        def _():
            pltpu.make_async_copy(zeros, out.at[j], out_sem).start()

    pltpu.make_async_copy(held, out, out_sem).wait()


def place(got, pick, valid):
    slots, block = got[0].shape[0], got[0].shape[1:]
    count = slots * CHUNKS
    return pl.pallas_call(
        place_kernel,
        out_shape=jax.ShapeDtypeStruct((count,) + block, got[0].dtype),
        in_specs=[pl.BlockSpec(memory_space=pltpu.SMEM)] * 2
        + [pl.BlockSpec(memory_space=pl.ANY)] * CHUNKS,
        out_specs=pl.BlockSpec(memory_space=pl.ANY),
        scratch_shapes=[
            pltpu.VMEM((count,) + block, got[0].dtype),
            pltpu.VMEM(block, got[0].dtype),
            pltpu.SemaphoreType.DMA((CHUNKS,)),
            pltpu.SemaphoreType.DMA,
        ],
    )(pick, valid, *got)


def shards(thinker_rows, proj_weight, proj_bias, cotangent, block_owner, block_offset):
    row_count, local_width = thinker_rows.shape
    width = proj_weight.shape[1]
    tensor_count = lax.axis_size("tensor")
    dp_count = lax.axis_size("dp")
    block_total = row_count // BLOCK
    per_chunk = block_total // CHUNKS
    share = per_chunk * BLOCK // tensor_count
    t = lax.axis_index("tensor")
    owner = block_owner.reshape(per_chunk, CHUNKS)
    offset = block_offset.reshape(per_chunk, CHUNKS)
    owners = jnp.arange(dp_count, dtype=jnp.int32)
    hot = owner[:, :, None] == owners[None, None, :]
    send_offset = jnp.sum(jnp.where(hot, offset[:, :, None] + 1, 0), axis=0) - 1
    got_offset = lax.all_to_all(send_offset.T, "dp", split_axis=0, concat_axis=0, tiled=True)
    rows4 = thinker_rows.reshape(per_chunk, CHUNKS, BLOCK, local_width)
    cot4 = cotangent.reshape(per_chunk, CHUNKS, BLOCK, width)
    per_block = BLOCK // share
    xs = [rows4[:, c].reshape(per_chunk * BLOCK, local_width) for c in range(CHUNKS)]
    weight_term = jnp.zeros((local_width, width), jnp.float32)
    got = []
    slopes = []
    last = None
    for c in range(CHUNKS):
        part = jnp.dot(xs[c], proj_weight, preferred_element_type=jnp.float32).astype(jnp.bfloat16)
        summed = lax.psum_scatter(part, "tensor", scatter_dimension=0, tiled=True).astype(jnp.float32)
        if last is not None:
            summed, last = lax.optimization_barrier((summed, last))
        own_cot = lax.dynamic_slice(
            cot4, (t // per_block, c, (t % per_block) * share, 0), (1, 1, share, width)
        ).reshape(share, width)
        last = slope_of(summed, proj_bias, own_cot)
        slopes.append(lax.all_gather(last, "tensor", axis=0, tiled=True))
    for c in range(CHUNKS):
        slope_rows = slopes[c]
        if c:
            slope_rows, got[-1], weight_term = lax.optimization_barrier((slope_rows, got[-1], weight_term))
        input_grad = lax.dot_general(
            slope_rows, proj_weight, (((1,), (1,)), ((), ())), preferred_element_type=jnp.float32
        ).astype(jnp.bfloat16).reshape(per_chunk, BLOCK, local_width)
        send = jnp.zeros((dp_count, BLOCK, local_width), jnp.bfloat16)
        for k in range(per_chunk):
            send = jnp.where(hot[k, c][:, None, None], input_grad[k][None], send)
        got.append(lax.all_to_all(send, "dp", split_axis=0, concat_axis=0, tiled=True))
        weight_term = weight_term + lax.dot_general(
            xs[c], slope_rows, (((0,), (0,)), ((), ())), preferred_element_type=jnp.float32
        )
    grad_scale = float(row_count * dp_count) ** (-0.5)
    proj_grad = lax.psum_scatter(
        (weight_term * grad_scale).astype(jnp.bfloat16), "dp", scatter_dimension=0, tiled=True
    ).astype(jnp.float32)
    slots = CHUNKS * dp_count
    flat_offset = got_offset.T.reshape(slots)
    match = flat_offset[None, :] == jnp.arange(2 * block_total, dtype=jnp.int32)[:, None]
    pick = jnp.sum(jnp.where(match, jnp.arange(slots, dtype=jnp.int32)[None, :], 0), axis=1)
    valid = jnp.any(match, axis=1).astype(jnp.int32)
    placed = place(got, pick, valid)
    return (placed.reshape(2 * row_count, local_width), proj_grad)


def solution(mesh):
    return jax.shard_map(
        shards,
        mesh=mesh,
        in_specs=(P("dp", "tensor"), P("tensor", None), P(), P("dp", None), P("dp"), P("dp")),
        out_specs=(P("dp", "tensor"), P(("tensor", "dp"), None)),
        check_vma=False,
    )
```

time: 353 us -> 608 us (1.72)
  waiting for transfers between devices: 253 us -> 452 us
  matrix products: 41 us -> 78.1 us
  starting transfers between devices: 10.1 us -> 26.8 us
  local copies, waits for them, and re-layouts: 25.6 us -> 14.1 us
  other arithmetic: 8.91 us -> 16.9 us
    reduce_scatter x1 -> x4, waiting for transfers between devices: 105 us -> 293 us  [shards(): lax.psum_scatter(part, 'tensor', scatter_dimension=0, tiled=True)]
    all_gather x1 -> x4, waiting for transfers between devices: 99.5 us -> 140 us  [shards(): slopes.append(lax.all_gather(last, 'tensor', axis=0, tiled=True))]
    all_to_all x2 -> x5, waiting for transfers between devices: 47.5 us -> 19.4 us  [the longest x4 19.4 us: shards(): lax.all_to_all(send, 'dp', split_axis=0, concat_axis=0, tiled=True)]
    dot_general x3 -> x8, matrix products: 28.5 us -> 56.1 us  [the longest x4 34.1 us: shards(): lax.dot_general(xs[c], slope_rows, (((0,), (0,)), ((), ())), preferred_el...]
    all_to_all x2 -> x5, starting transfers between devices: 9.94 us -> 26.5 us  [the longest x4 21.1 us: shards(): lax.all_to_all(send, 'dp', split_axis=0, concat_axis=0, tiled=True)]
    dot_general x1 -> x4, matrix products: 12.5 us -> 22 us  [shards(): lax.dot_general(slope_rows, proj_weight, (((1,), (1,)), ((), ())), prefer...]
    unnamed x14 -> x19, local copies, waits for them, and re-layouts: 15 us -> 11.1 us
  transfers between devices with their start and end apart: 5 -> 14, of which waited for: 3 -> 9; matrix products, arithmetic and copies ran while one was open for 10% -> 14% of each run, Pallas kernels for 0% -> 1%
where the time goes in v1:
time: 608 us; the launch traced here: 607 us
  waiting for transfers between devices  452 us (74%)
  matrix products  78.1 us (13%)
  starting transfers between devices  26.8 us (4%)
  other arithmetic  16.9 us (3%)
  local copies, waits for them, and re-layouts  14.1 us (2%)
  between operations  14 us (2%)
    reduce_scatter x4, waiting for transfers between devices, shards(): lax.psum_scatter(part, 'tensor', scatter_dimension=0, tiled=True)  293 us
    all_gather x4, waiting for transfers between devices, shards(): slopes.append(lax.all_gather(last, 'tensor', axis=0, tiled=True))  140 us
    dot_general x4, matrix products, shards(): lax.dot_general(xs[c], slope_rows, (((0,), (0,)), ((), ())), preferred_el...  34.1 us
    dot_general x4, matrix products, shards(): lax.dot_general(slope_rows, proj_weight, (((1,), (1,)), ((), ())), prefer...  22 us
    dot_general x4, matrix products, shards(): jnp.dot(xs[c], proj_weight, preferred_element_type=jnp.float32)  21.9 us
    all_to_all x4, starting transfers between devices, shards(): lax.all_to_all(send, 'dp', split_axis=0, concat_axis=0, tiled=True)  21.1 us
    all_to_all x4, waiting for transfers between devices, shards(): lax.all_to_all(send, 'dp', split_axis=0, concat_axis=0, tiled=True)  19.4 us
  transfers between devices with their start and end apart: 14, of which 9 were waited for; matrix products, arithmetic and copies ran while one was open for 14% of the time, Pallas kernels for 1%

profile of v1, /device:TPU:1, one launch (start us, length us, event | category | flops | bytes accessed | tf_op | source)
XLA Modules:
  0.0 607.3 jit_solution(14518701700161372783)
XLA Ops:
  7.2 0.0 reduce-scatter.10.cloned.1.call-start
  7.2 1.9 fusion.11
  9.1 0.8 copy-done.6
  9.9 3.9 convolution_convert_fusion.2
  13.8 0.0 reduce-scatter.8.cloned.1.call-start
  13.9 6.0 convolution_convert_fusion.3
  19.9 0.0 reduce-scatter.12.cloned.1.call-start
  20.0 5.9 convolution_convert_fusion.1
  25.9 0.0 reduce-scatter.14.cloned.1.call-start
  26.0 6.0 convolution_convert_fusion
  32.1 0.0 all-gather.7.cloned.1.call-start
  32.1 60.8 %reduce-scatter.10.cloned.1.call-done = bf16[32,3584]{1,0:T(8,128)(2,1)} async-done(((bf16[512,3584]{1,0:T(8,128)(2,1)}), bf16[32,3584]{1,0:T(8,128)(2,1)}) %reduce-scatter.10.cloned.1.call-update) | async-done | bytes 229392 | tf_op jit(solution)/shard_map/reduce_scatter | solution.py:89
  92.9 1.9 fusion.7
  94.9 0.0 all-gather.5.cloned.1.call-start
  94.9 78.2 %reduce-scatter.8.cloned.1.call-done = bf16[32,3584]{1,0:T(8,128)(2,1)} async-done(((bf16[512,3584]{1,0:T(8,128)(2,1)}), bf16[32,3584]{1,0:T(8,128)(2,1)}) %reduce-scatter.8.cloned.1.call-update) | async-done | bytes 229392 | tf_op jit(solution)/shard_map/reduce_scatter | solution.py:89
  173.1 1.0 convert_element_type.85
  174.1 1.8 fusion.9
  175.9 0.0 all-gather.9.cloned.1.call-start
  175.9 77.0 %reduce-scatter.12.cloned.1.call-done = bf16[32,3584]{1,0:T(8,128)(2,1)} async-done(((bf16[512,3584]{1,0:T(8,128)(2,1)}), bf16[32,3584]{1,0:T(8,128)(2,1)}) %reduce-scatter.12.cloned.1.call-update) | async-done | bytes 229392 | tf_op jit(solution)/shard_map/reduce_scatter | solution.py:89
  252.9 1.0 convert_element_type.96
  253.9 1.8 fusion.5
  255.8 0.0 all-gather.11.cloned.1.call-start
  255.8 77.1 %reduce-scatter.14.cloned.1.call-done = bf16[32,3584]{1,0:T(8,128)(2,1)} async-done(((bf16[512,3584]{1,0:T(8,128)(2,1)}), bf16[32,3584]{1,0:T(8,128)(2,1)}) %reduce-scatter.14.cloned.1.call-update) | async-done | bytes 229392 | tf_op jit(solution)/shard_map/reduce_scatter | solution.py:89
  332.9 1.0 convert_element_type.102
  333.9 1.8 fusion.3
  335.8 0.1 eq.35
  335.9 0.1 iota_compare_fusion.1
  336.0 49.6 %all-gather.7.cloned.1.call-done = bf16[512,3584]{1,0:T(8,128)(2,1)} async-done(((bf16[32,3584]{1,0:T(8,128)(2,1)}), bf16[512,3584]{1,0:T(8,128)(2,1)}) %all-gather.7.cloned.1.call-update) | async-done | bytes 3670032 | tf_op jit(solution)/shard_map/all_gather | solution.py:96
  385.6 5.2 convolution_convert_fusion.7
  390.9 1.3 select_select_fusion.3
  392.2 5.4 all-to-all-start.1
  397.6 7.1 %convolution_bitcast_fusion = f32[512,3584]{0,1:T(8,128)} fusion(bf16[512,3584]{1,0:T(8,128)(2,1)} %all-gather.7.cloned.1.call-done, bf16[512,512]{1,0:T(8,128)(2,1)S(1)} %bitcast.104), kind=kOutput, calls=%fused_computation.5 | convolution fusion | flops 1879048192 | bytes 11534336 | tf_op jit(solution)/shard_map/dot_general | solution.py:108
  404.7 31.6 %all-gather.5.cloned.1.call-done = bf16[512,3584]{1,0:T(8,128)(2,1)} async-done(((bf16[32,3584]{1,0:T(8,128)(2,1)}), bf16[512,3584]{1,0:T(8,128)(2,1)}) %all-gather.5.cloned.1.call-update) | async-done | bytes 3670032 | tf_op jit(solution)/shard_map/all_gather | solution.py:96
  436.3 5.6 convolution_convert_fusion.6
  442.0 1.3 select_select_fusion.2
  443.3 5.4 all-to-all-start.2
  448.7 9.2 %bitcast_add_fusion.2 = f32[512,3584]{0,1:T(8,128)} fusion(f32[512,3584]{0,1:T(8,128)} %convolution_bitcast_fusion, bf16[512,3584]{1,0:T(8,128)(2,1)} %all-gather.5.cloned.1.call-done, bf16[512,512]{1,0:T(8,128)(2,1)S(1)} %bitcast.102), kind=kOutput, calls=%fused_computation.4 | convolution fusion | flops 1880883200 | bytes 18874368 | tf_op jit(solution)/shard_map/dot_general | solution.py:108
  457.9 29.2 %all-gather.9.cloned.1.call-done = bf16[512,3584]{1,0:T(8,128)(2,1)} async-done(((bf16[32,3584]{1,0:T(8,128)(2,1)}), bf16[512,3584]{1,0:T(8,128)(2,1)}) %all-gather.9.cloned.1.call-update) | async-done | bytes 3670032 | tf_op jit(solution)/shard_map/all_gather | solution.py:96
  487.2 5.6 convolution_convert_fusion.5
  492.8 1.3 select_select_fusion.1
  494.1 5.4 all-to-all-start.3
  499.5 9.2 %bitcast_add_fusion.1 = f32[512,3584]{0,1:T(8,128)} fusion(f32[512,3584]{0,1:T(8,128)} %bitcast_add_fusion.2, bf16[512,3584]{1,0:T(8,128)(2,1)} %all-gather.9.cloned.1.call-done, bf16[512,512]{1,0:T(8,128)(2,1)S(1)} %bitcast.100), kind=kOutput, calls=%fused_computation.3 | convolution fusion | flops 1880883200 | bytes 18874368 | tf_op jit(solution)/shard_map/dot_general | solution.py:108
  508.8 29.2 %all-gather.11.cloned.1.call-done = bf16[512,3584]{1,0:T(8,128)(2,1)} async-done(((bf16[32,3584]{1,0:T(8,128)(2,1)}), bf16[512,3584]{1,0:T(8,128)(2,1)}) %all-gather.11.cloned.1.call-update) | async-done | bytes 3670032 | tf_op jit(solution)/shard_map/all_gather | solution.py:96
  538.0 8.5 %fusion.1 = bf16[512,3584]{0,1:T(8,128)(2,1)} fusion(f32[512,3584]{0,1:T(8,128)} %bitcast_add_fusion.1, bf16[512,3584]{1,0:T(8,128)(2,1)} %all-gather.11.cloned.1.call-done, bf16[512,512]{1,0:T(8,128)(2,1)S(1)} %bitcast.98), kind=kOutput, calls=%fused_computation.2 | convolution fusion | flops 1884553216 | bytes 15204352 | tf_op jit(solution)/shard_map/dot_general | solution.py:108
  546.5 6.0 copy.15
  552.5 0.6 copy-done.7
  553.1 0.1 add.104
  553.2 0.1 select_reduce_fusion.1
  553.3 0.7 copy.12
  554.0 5.4 all-to-all-start
  559.4 5.6 convolution_convert_fusion.4
  565.1 1.3 select_select_fusion
  566.4 4.8 all-to-all-start.4
  571.2 0.1 copy.13
  571.2 0.1 eq.39
  571.3 0.1 fusion.10
  571.5 0.6 convert_element_type.81.valid
  572.0 0.6 select_reduce_fusion.pick
  572.7 19.4 %all-to-all-done.4.refs_3_ = bf16[8,128,512]{2,1,0:T(8,128)(2,1)S(1)} async-done(((bf16[8,128,512]{2,1,0:T(8,128)(2,1)}), bf16[8,128,512]{2,1,0:T(8,128)(2,1)S(1)}, u32[]{:S(2)}, u32[]{:S(2)}) %all-to-all-start.4) | async-done | bytes 1048608 | tf_op jit(solution)/shard_map/all_to_all | solution.py:107
  592.1 1.0 copy-done.3
  593.1 4.9 shard_map.77
  598.0 0.0 reduce-scatter.16.cloned.1.call-done
  598.1 1.4 copy.16
  599.5 1.2 copy.14
  (34 shorter events, 0.4 us)
Async XLA Ops:
  7.2 85.7 %reduce-scatter.10.cloned.1.call-start = ((), (), s32[]{:S(2)}) async-start(), calls=%async_computation.11 | async-start | bytes 3899392 | tf_op jit(solution)/shard_map/reduce_scatter | solution.py:89
  7.2 2.7 copy-start.6
  13.8 159.3 %reduce-scatter.8.cloned.1.call-start = ((), (), s32[]{:S(2)}) async-start(), calls=%async_computation.10 | async-start | bytes 3899392 | tf_op jit(solution)/shard_map/reduce_scatter | solution.py:89
  19.9 233.0 %reduce-scatter.12.cloned.1.call-start = ((), (), s32[]{:S(2)}) async-start(), calls=%async_computation.14 | async-start | bytes 3899392 | tf_op jit(solution)/shard_map/reduce_scatter | solution.py:89
  25.9 307.0 %reduce-scatter.14.cloned.1.call-start = ((), (), s32[]{:S(2)}) async-start(), calls=%async_computation.16 | async-start | bytes 3899392 | tf_op jit(solution)/shard_map/reduce_scatter | solution.py:89
  32.0 60.9 %copy-start.4 = (f32[3584]{0:T(1024)S(1)}, f32[3584]{0:T(1024)}, u32[]{:S(2)}) copy-start(f32[3584]{0:T(1024)} %param.8) | copy-start | bytes 43012
  32.0 303.7 %copy-start.5 = (s32[16]{0:T(128)S(1)}, s32[16]{0:T(128)}, u32[]{:S(2)}) copy-start(s32[16]{0:T(128)} %param.10) | copy-start | bytes 196
  32.1 353.5 %all-gather.7.cloned.1.call-start = ((), (), s32[]{:S(2)}) async-start(), calls=%async_computation.13 | async-start | bytes 3899392 | tf_op jit(solution)/shard_map/all_gather | solution.py:96
  94.9 341.4 %all-gather.5.cloned.1.call-start = ((), (), s32[]{:S(2)}) async-start(), calls=%async_computation.12 | async-start | bytes 3899392 | tf_op jit(solution)/shard_map/all_gather | solution.py:96
  175.9 311.3 %all-gather.9.cloned.1.call-start = ((), (), s32[]{:S(2)}) async-start(), calls=%async_computation.15 | async-start | bytes 3899392 | tf_op jit(solution)/shard_map/all_gather | solution.py:96
  255.8 282.2 %all-gather.11.cloned.1.call-start = ((), (), s32[]{:S(2)}) async-start(), calls=%async_computation.17 | async-start | bytes 3899392 | tf_op jit(solution)/shard_map/all_gather | solution.py:96
  392.2 44.1 %all-to-all-start.1 = ((bf16[8,128,512]{2,1,0:T(8,128)(2,1)}), bf16[8,128,512]{2,1,0:T(8,128)(2,1)S(1)}, u32[]{:S(2)}, u32[]{:S(2)}) async-start(bf16[8,128,512]{2,1,0:T(8,128)(2,1)} %select_select_fusion.3), calls=%async_computation.3 | async-start | bytes 2097152 | tf_op jit(solution)/shard_map/all_to_all | solution.py:107
  436.3 5.6 copy-start
  443.3 43.9 %all-to-all-start.2 = ((bf16[8,128,512]{2,1,0:T(8,128)(2,1)}), bf16[8,128,512]{2,1,0:T(8,128)(2,1)S(1)}, u32[]{:S(2)}, u32[]{:S(2)}) async-start(bf16[8,128,512]{2,1,0:T(8,128)(2,1)} %select_select_fusion.2), calls=%async_computation.5 | async-start | bytes 2097152 | tf_op jit(solution)/shard_map/all_to_all | solution.py:107
  487.2 5.6 copy-start.1
  494.1 43.9 %all-to-all-start.3 = ((bf16[8,128,512]{2,1,0:T(8,128)(2,1)}), bf16[8,128,512]{2,1,0:T(8,128)(2,1)S(1)}, u32[]{:S(2)}, u32[]{:S(2)}) async-start(bf16[8,128,512]{2,1,0:T(8,128)(2,1)} %select_select_fusion.1), calls=%async_computation.7 | async-start | bytes 2097152 | tf_op jit(solution)/shard_map/all_to_all | solution.py:107
  499.5 98.5 %reduce-scatter.16.cloned.1.call-start = ((), (), s32[]{:S(2)}) async-start(), calls=%async_computation.18 | async-start | bytes 4128768
  538.0 8.5 %copy-start.2 = (bf16[8,128,512]{2,1,0:T(8,128)(2,1)}, bf16[8,128,512]{2,1,0:T(8,128)(2,1)S(1)}, u32[]{:S(2)}) copy-start(bf16[8,128,512]{2,1,0:T(8,128)(2,1)S(1)} %all-to-all-done.3.refs_2_) | copy-start | bytes 3145732
  552.5 0.7 copy-start.7
  554.0 12.4 %all-to-all-start = ((s32[8,1,4]{2,1,0:T(1,128)}), s32[8,1,4]{2,1,0:T(1,128)S(1)}, u32[]{:S(2)}, u32[]{:S(2)}) async-start(s32[8,1,4]{2,1,0:T(1,128)} %copy.12), calls=%async_computation | async-start | bytes 8192 | tf_op jit(solution)/shard_map/all_to_all | solution.py:78
  566.4 25.7 %all-to-all-start.4 = ((bf16[8,128,512]{2,1,0:T(8,128)(2,1)}), bf16[8,128,512]{2,1,0:T(8,128)(2,1)S(1)}, u32[]{:S(2)}, u32[]{:S(2)}) async-start(bf16[8,128,512]{2,1,0:T(8,128)(2,1)} %select_select_fusion), calls=%async_computation.8 | async-start | bytes 2097152 | tf_op jit(solution)/shard_map/all_to_all | solution.py:107
  592.1 1.0 copy-start.3
Sparse Core Ops, SparseCore 0:
  13.9 78.9 reduce-scatter.9
  96.3 76.7 reduce-scatter.7
  176.5 76.4 reduce-scatter.11
  256.2 76.7 reduce-scatter.13
  335.5 50.0 all-gather.6
  387.6 48.6 all-gather.4
  438.4 48.6 all-gather.8
  489.3 48.6 all-gather.10
  552.6 42.6 reduce-scatter.15

commit v2 on v0

v2 whole, which is shorter than its diff:
```python
import functools

import jax
import jax.numpy as jnp
from jax import lax
from jax.experimental import pallas as pl
from jax.experimental.pallas import tpu as pltpu
from jax.sharding import PartitionSpec as P

BLOCK = 128
CH = 4
N = 4
DP = 8
TILE = 16
FEAT = 512
WIDTH = 3584
HALF = WIDTH // 2
COL = 512
ROWS = N * BLOCK
MESH = pl.DeviceIdType.MESH
BF = jnp.bfloat16
F32 = jnp.float32
STEPS = (
    ("A", 0), ("R1", 0), ("A", 1), ("R1", 1), ("R2", 0), ("A", 3), ("R1", 3), ("A", 2), ("R1", 2), ("R2", 1),
    ("R3", 0), ("R2", 2), ("R5", 0), ("R2", 3), ("R3", 2), ("R3", 1), ("R6", 0), ("R5", 2), ("R3", 3), ("G2",
    0), ("R5", 1), ("R6", 2), ("G3", 0), ("R6", 1), ("G2", 2), ("G4", 0), ("G3", 2), ("G2", 1), ("D", 0),
    ("R5", 3), ("G4", 2), ("R6", 3), ("G3", 1), ("D", 2), ("W", 0), ("G2", 3), ("G4", 1), ("G3", 3), ("D", 1),
    ("W", 1), ("G4", 3), ("W", 2), ("D", 3), ("W", 3),
)


def main_kernel(
    owner, offset, bias, x_hbm, w_hbm, cot_hbm,
    got, got_info, grad_out,
    info, xv, xt, w, s, r1, r2, r4, out5, r5, cot, acc, gin, slots, pair, y1, y2,
    load_sem, cot_sem, send_sem, recv_sem, dp_send, dp_recv, own_sem, info_send, info_recv, gw_send, gw_recv,
):
    t = lax.axis_index("tensor")
    d = lax.axis_index("dp")
    z, x = t // N, t % N
    y, core = d // 2, d % 2

    def at(zz, xx):
        return {"tensor": (zz % N) * N + xx % N}

    def hop(axis, delta):
        return at(z, x + N + delta) if axis == 0 else at(z + N + delta, x)

    def peer(k):
        return {"dp": (d + k) % DP}

    def load_x(c):
        return pltpu.make_async_copy(x_hbm.at[:, c], xv.at[c], load_sem.at[c])

    def load_w():
        return pltpu.make_async_copy(w_hbm, w, load_sem.at[CH])

    def load_cot(c, h):
        return pltpu.make_async_copy(cot_hbm.at[x, c, h, z], cot.at[c, h], cot_sem.at[c, h])

    load_x(0).start()
    load_w().start()
    for c in range(1, CH):
        load_x(c).start()
    for c in range(CH):
        for h in range(2):
            load_cot(c, h).start()

    row = lax.broadcasted_iota(jnp.int32, (8, 128), 0)
    lane = lax.broadcasted_iota(jnp.int32, (8, 128), 1)
    table = jnp.zeros((8, 128), jnp.int32)
    for b in range(N * CH):
        table = jnp.where(lane == b, jnp.where(row == 0, owner[b], offset[b]), table)
    info[...] = table

    barrier = pltpu.get_barrier_semaphore()
    for axis in range(2):
        for delta in (1, -1):
            pl.semaphore_signal(barrier, inc=1, device_id=hop(axis, delta), device_id_type=MESH)
    for k in range(1, DP):
        pl.semaphore_signal(barrier, inc=1, device_id=peer(k), device_id_type=MESH)
    pl.semaphore_wait(barrier, 4 + DP - 1)

    def rows(ref, h, f, g):
        return ref.at[f, 0, g] if h == 0 else ref.at[g, 1, f]

    def copy(c, k, src, dst, dev):
        return pltpu.make_async_remote_copy(
            src_ref=src, dst_ref=dst, send_sem=send_sem.at[c, k], recv_sem=recv_sem.at[c, k],
            device_id=dev, device_id_type=MESH,
        )

    def first(h):
        return (x, z, 0, 1) if h == 0 else (z, x, 1, 0)

    LOW, HIGH, ALL = pl.ds(0, 2), pl.ds(2, 2), pl.ds(0, 4)
    CL, CR = pl.ds(0, HALF), pl.ds(HALF, HALF)

    def rs1(c, h, e):
        i, j, a, b = first(h)
        return copy(c, 2 * h + e, rows(s.at[c], h, (i + 2) % N, (LOW, HIGH)[e]), r1.at[c, h, e], hop(a, (1, -1)[e]))

    def rs2(c, h, e):
        i, j, a, b = first(h)
        return copy(c, 4 + 2 * h + e, rows(s.at[c], h, (i + (1, 3)[e]) % N, ALL), r2.at[c, h, e], hop(a, (1, -1)[e]))

    def rs4(c, h, e):
        i, j, a, b = first(h)
        return copy(c, 8 + 2 * h + e, rows(s.at[c], h, i, (j + 2) % N).at[:, (CL, CR)[e]], r4.at[c, h, e], hop(b, (1, -1)[e]))

    def rs5(c, h, e):
        i, j, a, b = first(h)
        return copy(c, 12 + 2 * h + e, out5.at[c, h, e], r5.at[c, h, e], hop(b, (1, -1)[e]))

    def ag1(c, h, e, landing=False):
        i, j, a, b = first(h)
        part = rows(s.at[c], h, i, (j + (3, 1)[e]) % N if landing else j)
        return copy(c, 16 + 2 * h + e, part, part, hop(b, (1, -1)[e]))

    def ag2(c, h, e, landing=False):
        i, j, a, b = first(h)
        part = rows(s.at[c], h, i, (j + 2) % N if landing else (j + (3, 1)[e]) % N).at[:, (CL, CR)[e]]
        return copy(c, 20 + 2 * h + e, part, part, hop(b, (1, -1)[e]))

    def ag3(c, h, e, landing=False):
        i, j, a, b = first(h)
        part = rows(s.at[c], h, (i + (3, 1)[e]) % N if landing else i, ALL)
        return copy(c, 24 + 2 * h + e, part, part, hop(a, (1, -1)[e]))

    def ag4(c, h, e, landing=False):
        i, j, a, b = first(h)
        part = rows(s.at[c], h, (i + 2) % N if landing else (i + (3, 1)[e]) % N, (LOW, HIGH)[e])
        return copy(c, 28 + 2 * h + e, part, part, hop(a, (1, -1)[e]))

    BOTH = [(h, e) for e in range(2) for h in range(2)]

    def matmul(c):
        if c == 0:
            load_w().wait()
        load_x(c).wait()

        @pl.loop(0, WIDTH // COL)
        def _(n):
            cols = pl.ds(pl.multiple_of(n * COL, COL), COL)
            out = jnp.dot(xv[c].reshape(ROWS, FEAT), w[:, cols], preferred_element_type=F32).astype(BF)
            s[c, :, :, :, :, cols] = out.reshape(N, 2, N, TILE, COL)

    def add(dst, src):
        dst[...] = (dst[...].astype(F32) + src[...].astype(F32)).astype(BF)

    def reduce1(c):
        for h, e in BOTH:
            rs1(c, h, e).start()

    def reduce2(c):
        for h, e in BOTH:
            i, j, a, b = first(h)
            rs1(c, h, e).wait_recv()
            f = (i + (1, 3)[e]) % N

            @pl.loop(0, 2)
            def _(g):
                add(rows(s.at[c], h, f, 2 * e + g), r1.at[c, h, e, g])

            rs2(c, h, e).start()

    def reduce3(c):
        for h in range(2):
            i, j, a, b = first(h)
            for e in range(2):
                rs2(c, h, e).wait_recv()

            @pl.loop(0, N)
            def _(g):
                own = rows(s.at[c], h, i, g)
                own[...] = (
                    own[...].astype(F32) + r2[c, h, 0, g].astype(F32) + r2[c, h, 1, g].astype(F32)
                ).astype(BF)

            for e in range(2):
                rs4(c, h, e).start()

    def reduce5(c):
        for make in (rs1, rs2, rs4):
            for h, e in BOTH:
                make(c, h, e).wait_send()
        for h, e in BOTH:
            i, j, a, b = first(h)
            part = rows(s.at[c], h, i, (j + (1, 3)[e]) % N)
            mine, other = ((CL, CR), (CR, CL))[e]
            out5[c, h, e, :, other] = part[:, other]
            rs4(c, h, e).wait_recv()
            out5[c, h, e, :, mine] = (part[:, mine].astype(F32) + r4[c, h, e].astype(F32)).astype(BF)
            rs5(c, h, e).start()

    def reduce6(c):
        for h in range(2):
            i, j, a, b = first(h)
            for e in range(2):
                rs5(c, h, e).wait_recv()
            load_cot(c, h).wait()

            @pl.loop(0, WIDTH // COL)
            def _(n):
                cols = pl.ds(pl.multiple_of(n * COL, COL), COL)
                own = rows(s.at[c], h, i, j)
                total = own[:, cols].astype(F32) + r5[c, h, 0, :, cols].astype(F32) + r5[c, h, 1, :, cols].astype(F32)
                pre = total + bias[cols][None, :]
                gate = 1.0 / (1.0 + jnp.exp(-pre))
                slope = cot[c, h, :, cols].astype(F32) * gate * (1.0 + pre * (1.0 - gate))
                rows(s.at[c], h, i, j)[:, cols] = slope.astype(BF)

            for e in range(2):
                ag1(c, h, e).start()

    def gather2(c):
        for h, e in BOTH:
            ag1(c, h, e, True).wait_recv()
            ag2(c, h, e).start()

    def gather3(c):
        for h in range(2):
            for e in range(2):
                ag2(c, h, e, True).wait_recv()
            for e in range(2):
                ag3(c, h, e).start()

    def gather4(c):
        for h, e in BOTH:
            ag3(c, h, e, True).wait_recv()
            ag4(c, h, e).start()

    def slot_copy(c, k):
        return pltpu.make_async_remote_copy(
            src_ref=slots.at[c, k], dst_ref=got.at[c, d], send_sem=dp_send.at[c, k], recv_sem=dp_recv.at[c, k],
            device_id=peer(k), device_id_type=MESH,
        )

    def slot_landing(c, k):
        return pltpu.make_async_remote_copy(
            src_ref=slots.at[c, k], dst_ref=got.at[c, (d + DP - k) % DP], send_sem=dp_send.at[c, k],
            recv_sem=dp_recv.at[c, k], device_id=peer(k), device_id_type=MESH,
        )

    def own_slot(c):
        return pltpu.make_async_copy(slots.at[c, 0], got.at[c, d], own_sem.at[c])

    def sent(c):
        for make in (rs5, ag1, ag2, ag3, ag4):
            for h, e in BOTH:
                make(c, h, e).wait_send()

    def landed(c, name):
        other = ("D" if name == "W" else "W", c)
        if STEPS.index((name, c)) < STEPS.index(other):
            for h, e in BOTH:
                ag4(c, h, e, True).wait_recv()

    def data_grad(c):
        landed(c, "D")

        @pl.loop(0, 2)
        def _(n):
            half = FEAT // 2
            features = pl.ds(pl.multiple_of(n * half, half), half)
            out = lax.dot_general(
                s[c].reshape(ROWS, WIDTH), w[features, :], (((1,), (1,)), ((), ())), preferred_element_type=F32
            ).astype(BF)
            gin[:, :, features] = out.reshape(N, BLOCK, half)

        for k in range(DP):
            target = (d + k) % DP
            pick = jnp.int32(0)
            for b in range(1, N):
                pick = jnp.where(owner[b * CH + c] == target, b, pick)
            slots[c, k] = gin[pick]
            if k:
                slot_copy(c, k).start()
            else:
                own_slot(c).start()

    def weight_grad(c):
        landed(c, "W")
        place = [b for name, b in STEPS if name == "W"].index(c)
        if place == CH - 1:
            sent(0)
        xt[...] = xv[c].reshape(ROWS, FEAT).T

        @pl.loop(0, WIDTH // COL)
        def _(n):
            cols = pl.ds(pl.multiple_of(n * COL, COL), COL)
            part = s[c, :, :, :, :, cols].reshape(ROWS, COL)
            out = jnp.dot(xt[...], part, preferred_element_type=F32)
            if place == 0:
                acc[:, cols] = out
            elif place < CH - 1:
                acc[:, cols] += out
            else:
                full = ((acc[:, cols] + out) * (float(ROWS * CH * DP) ** -0.5)).astype(BF)
                s[0, :, :, :, :, cols] = full.reshape(N, 2, N, TILE, COL)

    def info_copy(k):
        return pltpu.make_async_remote_copy(
            src_ref=info, dst_ref=got_info.at[d], send_sem=info_send.at[k], recv_sem=info_recv.at[k],
            device_id=peer(k), device_id_type=MESH,
        )

    def info_landing(k):
        return pltpu.make_async_remote_copy(
            src_ref=info, dst_ref=got_info.at[(d + DP - k) % DP], send_sem=info_send.at[k], recv_sem=info_recv.at[k],
            device_id=peer(k), device_id_type=MESH,
        )

    own_info = pltpu.make_async_copy(info, got_info.at[d], info_send.at[0])
    own_info.start()
    for k in range(1, DP):
        info_copy(k).start()

    phases = {
        "A": matmul, "R1": reduce1, "R2": reduce2, "R3": reduce3, "R5": reduce5, "R6": reduce6,
        "G2": gather2, "G3": gather3, "G4": gather4, "D": data_grad, "W": weight_grad,
    }
    for name, c in STEPS:
        phases[name](c)

    def gw(k, src, dst, dev):
        return pltpu.make_async_remote_copy(
            src_ref=src, dst_ref=dst, send_sem=gw_send.at[k], recv_sem=gw_recv.at[k],
            device_id=dev, device_id_type=MESH,
        )

    sibling = {"dp": 2 * y + 1 - core}
    ring = [{"dp": (d + 2) % DP}, {"dp": (d + DP - 2) % DP}]
    swap = gw(0, s.at[0, :, 1 - core], pair, sibling)
    swap.start()
    swap.wait_recv()

    @pl.loop(0, N)
    def _(k):
        @pl.loop(0, N)
        def _(g):
            add(s.at[0, k, core, g], pair.at[k, g])

    step1 = [gw(1 + e, s.at[0, (y + 2) % N, core, (LOW, HIGH)[e]], y1.at[e], ring[e]) for e in range(2)]
    step2 = [gw(3 + e, s.at[0, (y + (1, 3)[e]) % N, core], y2.at[e], ring[e]) for e in range(2)]
    for e in range(2):
        step1[e].start()
    for e in range(2):
        step1[e].wait_recv()

        @pl.loop(0, 2)
        def _(g):
            add(s.at[0, (y + (1, 3)[e]) % N, core, 2 * e + g], y1.at[e, g])

        step2[e].start()
    for e in range(2):
        step2[e].wait_recv()

    @pl.loop(0, N)
    def _(g):
        grad_out[g] = s[0, y, core, g].astype(F32) + y2[0, g].astype(F32) + y2[1, g].astype(F32)

    swap.wait_send()
    for e in range(2):
        step1[e].wait_send()
        step2[e].wait_send()
    own_info.wait()
    for k in range(1, DP):
        info_copy(k).wait_send()
        info_landing(k).wait_recv()
    for c in range(CH):
        if c:
            sent(c)
        own_slot(c).wait()
        for k in range(1, DP):
            slot_copy(c, k).wait_send()
            slot_landing(c, k).wait_recv()


def place_kernel(me, info, got, grad, out, grad_out, table, held, zeros, passed, flag, info_sem, in_sem, grad_sem, out_sem):
    fetch = pltpu.make_async_copy(info, table, info_sem)
    fetch.start()
    load = pltpu.make_async_copy(got, held, in_sem)
    load.start()
    take = pltpu.make_async_copy(grad, passed, grad_sem)
    take.start()
    zeros[...] = jnp.zeros_like(zeros)
    count = out.shape[0]
    for j in range(count):
        flag[j] = 0
    fetch.wait()
    load.wait()
    take.wait()
    give = pltpu.make_async_copy(passed, grad_out, grad_sem)
    give.start()
    mine = me[0]
    for source in range(DP):
        for b in range(N):
            for c in range(CH):

                @pl.when(table[source, 0, b * CH + c] == mine)
                def _():
                    row = table[source, 1, b * CH + c]
                    flag[row] = 1
                    pltpu.make_async_copy(held.at[c, source], out.at[row], out_sem).start()

    for j in range(count):

        @pl.when(flag[j] == 0)
        def _():
            pltpu.make_async_copy(zeros, out.at[j], out_sem).start()

    pltpu.make_async_copy(out, out, out_sem).wait()
    give.wait()


def shards(thinker_rows, proj_weight, proj_bias, cotangent, block_owner, block_offset):
    vmem = pl.BlockSpec(memory_space=pltpu.VMEM)
    smem = pl.BlockSpec(memory_space=pltpu.SMEM)
    hbm = pl.BlockSpec(memory_space=pl.ANY)
    tile = (TILE, WIDTH)
    dma = pltpu.SemaphoreType.DMA
    got, got_info, grad = pl.pallas_call(
        main_kernel,
        out_shape=(
            jax.ShapeDtypeStruct((CH, DP, BLOCK, FEAT), BF),
            jax.ShapeDtypeStruct((DP, 8, 128), jnp.int32),
            jax.ShapeDtypeStruct((N,) + tile, F32),
        ),
        in_specs=[smem, smem, vmem, hbm, hbm, hbm],
        out_specs=(hbm, hbm, vmem),
        scratch_shapes=[
            pltpu.VMEM((8, 128), jnp.int32),
            pltpu.VMEM((CH, N, BLOCK, FEAT), BF),
            pltpu.VMEM((FEAT, ROWS), BF),
            pltpu.VMEM((FEAT, WIDTH), BF),
            pltpu.VMEM((CH, N, 2, N) + tile, BF),
            pltpu.VMEM((CH, 2, 2, 2) + tile, BF),
            pltpu.VMEM((CH, 2, 2, N) + tile, BF),
            pltpu.VMEM((CH, 2, 2, TILE, HALF), BF),
            pltpu.VMEM((CH, 2, 2) + tile, BF),
            pltpu.VMEM((CH, 2, 2) + tile, BF),
            pltpu.VMEM((CH, 2) + tile, BF),
            pltpu.VMEM((FEAT, WIDTH), F32),
            pltpu.VMEM((N, BLOCK, FEAT), BF),
            pltpu.VMEM((CH, DP, BLOCK, FEAT), BF),
            pltpu.VMEM((N, N) + tile, BF),
            pltpu.VMEM((2, 2) + tile, BF),
            pltpu.VMEM((2, N) + tile, BF),
            dma((CH + 1,)),
            dma((CH, 2)),
            dma((CH, 32)),
            dma((CH, 32)),
            dma((CH, DP)),
            dma((CH, DP)),
            dma((CH,)),
            dma((DP,)),
            dma((DP,)),
            dma((5,)),
            dma((5,)),
        ],
        compiler_params=pltpu.CompilerParams(
            collective_id=0, has_side_effects=True, vmem_limit_bytes=67_000_000
        ),
        name="fused_backward",
    )(
        block_owner,
        block_offset,
        proj_bias,
        thinker_rows.reshape(N, CH, BLOCK, FEAT),
        proj_weight,
        cotangent.reshape(N, CH, 2, N, TILE, WIDTH),
    )
    placed, grad = pl.pallas_call(
        place_kernel,
        out_shape=(
            jax.ShapeDtypeStruct((CH * DP, BLOCK, FEAT), BF),
            jax.ShapeDtypeStruct((N,) + tile, F32),
        ),
        in_specs=[smem, hbm, hbm, hbm],
        out_specs=(hbm, hbm),
        scratch_shapes=[
            pltpu.SMEM((DP, 8, 128), jnp.int32),
            pltpu.VMEM((CH, DP, BLOCK, FEAT), BF),
            pltpu.VMEM((BLOCK, FEAT), BF),
            pltpu.VMEM((N,) + tile, F32),
            pltpu.SMEM((CH * DP,), jnp.int32),
            dma,
            dma,
            dma,
            dma,
        ],
        name="place_blocks",
    )(lax.axis_index("dp").reshape(1), got_info, got, grad)
    return (placed.reshape(CH * DP * BLOCK, FEAT), grad.reshape(N * TILE, WIDTH))


def solution(mesh):
    return jax.shard_map(
        shards,
        mesh=mesh,
        in_specs=(P("dp", "tensor"), P("tensor", None), P(), P("dp", None), P("dp"), P("dp")),
        out_specs=(P("dp", "tensor"), P(("tensor", "dp"), None)),
        check_vma=False,
    )
```

time: 353 us -> 202 us (0.57)
  waiting for transfers between devices: 253 us -> 0 us
  Pallas kernels: 0 us -> 201 us
  matrix products: 41 us -> 0 us
  local copies, waits for them, and re-layouts: 25.6 us -> 0 us
  between operations: 13.8 us -> 0.64 us
  starting transfers between devices: 10.1 us -> 0 us
  other arithmetic: 8.91 us -> 0 us
    pallas_call x0 -> x2, Pallas kernels: none -> 201 us  [the longest x1 196 us: shards(): pl.pallas_call(main_kernel, out_shape=(jax.ShapeDtypeStruct((CH, DP, BLOC...]
    reduce_scatter x1 -> x0, waiting for transfers between devices: 105 us -> none  [shards(): lax.psum_scatter(jnp.dot(thinker_rows, proj_weight, preferred_element_typ...]
    all_gather x1 -> x0, waiting for transfers between devices: 99.5 us -> none  [shards(): lax.all_gather(slope_of(summed, proj_bias, own_cot), 'tensor', axis=0, ti...]
    all_to_all x2 -> x0, waiting for transfers between devices: 47.5 us -> none  [the longest x1 47.5 us: return_rows(): lax.all_to_all(send_rows, 'dp', split_axis=0, concat_axis=0, tiled=True)]
    dot_general x4 -> x0, matrix products: 41 us -> none  [the longest x1 13 us: shards(): jnp.dot(thinker_rows, proj_weight, preferred_element_type=jnp.float32)]
    unnamed x14 -> x0, local copies, waits for them, and re-layouts: 15 us -> none
    all_to_all x2 -> x0, starting transfers between devices: 9.94 us -> none  [the longest x1 5.13 us: return_rows(): lax.all_to_all(send_offset, 'dp', split_axis=0, concat_axis=0, tiled=True)]
    reshape x1 -> x0, local copies, waits for them, and re-layouts: 5.77 us -> none  [return_rows(): owner_grad.astype(jnp.bfloat16)]
  transfers between devices with their start and end apart: 5 -> 0, of which waited for: 3 -> 0; matrix products, arithmetic and copies ran while one was open for 10% -> 0% of each run, Pallas kernels for 0% -> 0%
where the time goes in v2:
time: 202 us; the launch traced here: 201 us
  Pallas kernels  201 us (100%)
    pallas_call x1, Pallas kernels, shards(): pl.pallas_call(main_kernel, out_shape=(jax.ShapeDtypeStruct((CH, DP, BLOC...  196 us
    pallas_call x1, Pallas kernels, shards(): pl.pallas_call(place_kernel, out_shape=(jax.ShapeDtypeStruct((CH * DP, BL...  4.76 us

profile of v2, /device:TPU:1, one launch (start us, length us, event | category | flops | bytes accessed | tf_op | source)
XLA Modules:
  0.0 201.4 jit_solution(37580937227641142)
XLA Ops:
  0.6 196.0 %fused_backward.1 = (bf16[4,8,128,512]{3,2,1,0:T(8,128)(2,1)}, s32[8,8,128]{2,1,0:T(8,128)}, f32[4,16,3584]{2,1,0:T(8,128)}) custom-call(s32[16]{0:T(128)} %owner.1, s32[16]{0:T(128)} %offset.1, f32[3584]{0:T(1024)} %bias.1, bf16[4,4,128,512]{3,2,1,0:T(8,128)(2,1)} %bitcast.6, bf16[512,3584]{1,0:T(8,128)(2,1)} %w_hbm.1, bf16[4,4,2,4,16,3584]{5,4,3,2,1,0:T(8,128)(2,1)} %bitcast.5), custom_call_target="tpu_custom_call" | custom-call | tf_op jit(solution)/shard_map/fused_backward/pallas_call | solution.py:423
  196.6 4.8 %place_blocks.1 = (bf16[32,128,512]{2,1,0:T(8,128)(2,1)}, f32[4,16,3584]{2,1,0:T(8,128)}) custom-call(s32[1]{0:T(128)} %bitcast.me, s32[8,8,128]{2,1,0:T(8,128)} %get-tuple-element.7.info, bf16[4,8,128,512]{3,2,1,0:T(8,128)(2,1)} %get-tuple-element.8.got, f32[4,16,3584]{2,1,0:T(8,128)} %get-tuple-element.9.grad), custom_call_target="tpu_custom_call" | custom-call | tf_op jit(solution)/shard_map/place_blocks/pallas_call | solution.py:474

commit v3 on v2

--- a/solution.py
+++ b/solution.py
@@ -9,30 +9,38 @@
 
 BLOCK = 128
 CH = 4
+PARTS = 2
+ALL_CH = CH * PARTS
 N = 4
 DP = 8
 TILE = 16
 FEAT = 512
 WIDTH = 3584
-HALF = WIDTH // 2
-COL = 512
+PART = WIDTH // PARTS
+HALF = PART // 2
+COL = 256
 ROWS = N * BLOCK
 MESH = pl.DeviceIdType.MESH
 BF = jnp.bfloat16
 F32 = jnp.float32
 STEPS = (
-    ("A", 0), ("R1", 0), ("A", 1), ("R1", 1), ("R2", 0), ("A", 3), ("R1", 3), ("A", 2), ("R1", 2), ("R2", 1),
-    ("R3", 0), ("R2", 2), ("R5", 0), ("R2", 3), ("R3", 2), ("R3", 1), ("R6", 0), ("R5", 2), ("R3", 3), ("G2",
-    0), ("R5", 1), ("R6", 2), ("G3", 0), ("R6", 1), ("G2", 2), ("G4", 0), ("G3", 2), ("G2", 1), ("D", 0),
-    ("R5", 3), ("G4", 2), ("R6", 3), ("G3", 1), ("D", 2), ("W", 0), ("G2", 3), ("G4", 1), ("G3", 3), ("D", 1),
-    ("W", 1), ("G4", 3), ("W", 2), ("D", 3), ("W", 3),
+    ("A", 1), ("R1", 1), ("A", 0), ("R1", 0), ("A", 3), ("R1", 3), ("A", 5), ("R1", 5), ("R2", 0), ("A", 6),
+    ("R2", 3), ("R3", 0), ("R2", 1), ("A", 2), ("A", 4), ("R5", 0), ("R1", 2), ("R1", 6), ("R3", 3), ("R2", 5),
+    ("R3", 1), ("R5", 3), ("R6", 0), ("R1", 4), ("R2", 2), ("R5", 1), ("R2", 4), ("A", 7), ("R3", 2), ("R6", 3),
+    ("R2", 6), ("G2", 3), ("R3", 4), ("R5", 2), ("R6", 1), ("G2", 0), ("G3", 3), ("G2", 1), ("G3", 0),
+    ("R5", 4), ("R6", 2), ("G4", 0), ("G3", 1), ("R6", 4), ("R3", 6), ("G2", 2), ("R3", 5), ("G4", 3),
+    ("G2", 4), ("R5", 6), ("R5", 5), ("R1", 7), ("G3", 2), ("R6", 5), ("W", 0), ("DL", 3), ("G4", 1), ("W", 3),
+    ("G4", 2), ("G3", 4), ("W", 1), ("G2", 5), ("R2", 7), ("W", 2), ("Y1", 0), ("G4", 4), ("R6", 6), ("R3", 7),
+    ("G3", 5), ("Y2", 0), ("D", 0), ("R5", 7), ("G2", 6), ("G4", 5), ("R6", 7), ("G3", 6), ("D", 1), ("Y3", 0),
+    ("G2", 7), ("G4", 6), ("W", 5), ("G3", 7), ("D", 2), ("G4", 7), ("W", 6), ("W", 4), ("W", 7), ("D", 3),
+    ("Y1", 1), ("Y2", 1), ("Y3", 1),
 )
 
 
 def main_kernel(
     owner, offset, bias, x_hbm, w_hbm, cot_hbm,
     got, got_info, grad_out,
-    info, xv, xt, w, s, r1, r2, r4, out5, r5, cot, acc, gin, slots, pair, y1, y2,
+    info, xv, xt, w, s, r1, r2, r4, out5, r5, cot, acc, left, gin, slots, stage, pair, y1, y2,
     load_sem, cot_sem, send_sem, recv_sem, dp_send, dp_recv, own_sem, info_send, info_recv, gw_send, gw_recv,
 ):
     t = lax.axis_index("tensor")
@@ -52,17 +60,24 @@
     def load_x(c):
         return pltpu.make_async_copy(x_hbm.at[:, c], xv.at[c], load_sem.at[c])
 
-    def load_w():
-        return pltpu.make_async_copy(w_hbm, w, load_sem.at[CH])
+    def load_w(part):
+        cols = pl.ds(part * PART, PART)
+        return pltpu.make_async_copy(w_hbm.at[:, cols], w.at[:, cols], load_sem.at[CH + part])
 
     def load_cot(c, h):
-        return pltpu.make_async_copy(cot_hbm.at[x, c, h, z], cot.at[c, h], cot_sem.at[c, h])
-
-    load_x(0).start()
-    load_w().start()
-    for c in range(1, CH):
+        src = cot_hbm.at[x, c % CH, h, z].at[:, pl.ds(c // CH * PART, PART)]
+        return pltpu.make_async_copy(src, cot.at[c, h], cot_sem.at[c, h])
+
+    arrivals = []
+    for name, c in STEPS:
+        if name == "A" and c % CH not in arrivals:
+            arrivals.append(c % CH)
+    load_x(arrivals[0]).start()
+    load_w(0).start()
+    for c in arrivals[1:]:
         load_x(c).start()
-    for c in range(CH):
+    load_w(1).start()
+    for c in range(ALL_CH):
         for h in range(2):
             load_cot(c, h).start()
 
@@ -134,16 +149,22 @@
 
     BOTH = [(h, e) for e in range(2) for h in range(2)]
 
+    def tile(base, n):
+        return pl.ds(pl.multiple_of(base + n * COL, COL), COL)
+
     def matmul(c):
-        if c == 0:
-            load_w().wait()
-        load_x(c).wait()
-
-        @pl.loop(0, WIDTH // COL)
+        rc, base = c % CH, c // CH * PART
+        if base not in loaded:
+            loaded.add(base)
+            load_w(c // CH).wait()
+        if ("x", rc) not in loaded:
+            loaded.add(("x", rc))
+            load_x(rc).wait()
+
+        @pl.loop(0, PART // COL)
         def _(n):
-            cols = pl.ds(pl.multiple_of(n * COL, COL), COL)
-            out = jnp.dot(xv[c].reshape(ROWS, FEAT), w[:, cols], preferred_element_type=F32).astype(BF)
-            s[c, :, :, :, :, cols] = out.reshape(N, 2, N, TILE, COL)
+            out = jnp.dot(xv[rc].reshape(ROWS, FEAT), w[:, tile(base, n)], preferred_element_type=F32).astype(BF)
+            s[c, :, :, :, :, tile(0, n)] = out.reshape(N, 2, N, TILE, COL)
 
     def add(dst, src):
         dst[...] = (dst[...].astype(F32) + src[...].astype(F32)).astype(BF)
@@ -200,12 +221,12 @@
                 rs5(c, h, e).wait_recv()
             load_cot(c, h).wait()
 
-            @pl.loop(0, WIDTH // COL)
+            @pl.loop(0, PART // COL)
             def _(n):
-                cols = pl.ds(pl.multiple_of(n * COL, COL), COL)
+                cols = tile(0, n)
                 own = rows(s.at[c], h, i, j)
                 total = own[:, cols].astype(F32) + r5[c, h, 0, :, cols].astype(F32) + r5[c, h, 1, :, cols].astype(F32)
-                pre = total + bias[cols][None, :]
+                pre = total + bias[tile(c // CH * PART, n)][None, :]
                 gate = 1.0 / (1.0 + jnp.exp(-pre))
                 slope = cot[c, h, :, cols].astype(F32) * gate * (1.0 + pre * (1.0 - gate))
                 rows(s.at[c], h, i, j)[:, cols] = slope.astype(BF)
@@ -250,23 +271,41 @@
             for h, e in BOTH:
                 make(c, h, e).wait_send()
 
-    def landed(c, name):
-        other = ("D" if name == "W" else "W", c)
-        if STEPS.index((name, c)) < STEPS.index(other):
+    def landed(c):
+        if c not in seen:
+            seen.add(c)
             for h, e in BOTH:
                 ag4(c, h, e, True).wait_recv()
 
-    def data_grad(c):
-        landed(c, "D")
+    def feature_tile(n):
+        half = FEAT // 2
+        return pl.ds(pl.multiple_of(n * half, half), half)
+
+    def grad_part(c, n):
+        cols = pl.ds(c // CH * PART, PART)
+        return lax.dot_general(
+            s[c].reshape(ROWS, PART), w[feature_tile(n), cols], (((1,), (1,)), ((), ())), preferred_element_type=F32
+        )
+
+    def data_grad_left(c):
+        landed(c)
 
         @pl.loop(0, 2)
         def _(n):
-            half = FEAT // 2
-            features = pl.ds(pl.multiple_of(n * half, half), half)
-            out = lax.dot_general(
-                s[c].reshape(ROWS, WIDTH), w[features, :], (((1,), (1,)), ((), ())), preferred_element_type=F32
-            ).astype(BF)
-            gin[:, :, features] = out.reshape(N, BLOCK, half)
+            left[:, feature_tile(n)] = grad_part(c, n)
+
+    def data_grad(c):
+        landed(c)
+        landed(c + CH)
+
+        @pl.loop(0, 2)
+        def _(n):
+            if ("DL", c) in STEPS:
+                out = left[:, feature_tile(n)]
+            else:
+                out = grad_part(c, n)
+            out = (out + grad_part(c + CH, n)).astype(BF)
+            gin[:, :, feature_tile(n)] = out.reshape(N, BLOCK, FEAT // 2)
 
         for k in range(DP):
             target = (d + k) % DP
@@ -280,24 +319,83 @@
                 own_slot(c).start()
 
     def weight_grad(c):
-        landed(c, "W")
-        place = [b for name, b in STEPS if name == "W"].index(c)
-        if place == CH - 1:
-            sent(0)
-        xt[...] = xv[c].reshape(ROWS, FEAT).T
-
-        @pl.loop(0, WIDTH // COL)
+        landed(c)
+        rc, part = c % CH, c // CH
+        place = [b for name, b in STEPS if name == "W" and b // CH == part].index(c)
+        if rc not in turned:
+            turned.add(rc)
+            xt[rc] = xv[rc].reshape(ROWS, FEAT).T
+
+        @pl.loop(0, PART // COL)
         def _(n):
-            cols = pl.ds(pl.multiple_of(n * COL, COL), COL)
-            part = s[c, :, :, :, :, cols].reshape(ROWS, COL)
-            out = jnp.dot(xt[...], part, preferred_element_type=F32)
+            rows_here = s[c, :, :, :, :, tile(0, n)].reshape(ROWS, COL)
+            out = jnp.dot(xt[rc], rows_here, preferred_element_type=F32)
+            cols = tile(part * PART, n)
             if place == 0:
                 acc[:, cols] = out
             elif place < CH - 1:
                 acc[:, cols] += out
             else:
                 full = ((acc[:, cols] + out) * (float(ROWS * CH * DP) ** -0.5)).astype(BF)
-                s[0, :, :, :, :, cols] = full.reshape(N, 2, N, TILE, COL)
+                stage[:, :, :, :, tile(0, n)] = full.reshape(N, 2, N, TILE, COL)
+
+        if place == CH - 1:
+            swap(part).start()
+
+    def gw(part, k, src, dst, dev):
+        return pltpu.make_async_remote_copy(
+            src_ref=src, dst_ref=dst, send_sem=gw_send.at[part, k], recv_sem=gw_recv.at[part, k],
+            device_id=dev, device_id_type=MESH,
+        )
+
+    def swap(part):
+        return gw(part, 0, stage.at[:, 1 - core], pair.at[part], {"dp": 2 * y + 1 - core})
+
+    def ring(e):
+        return {"dp": (d + (2, DP - 2)[e]) % DP}
+
+    def ring1(part, e):
+        return gw(part, 1 + e, stage.at[(y + 2) % N, core, (LOW, HIGH)[e]], y1.at[part, e], ring(e))
+
+    def ring2(part, e):
+        return gw(part, 3 + e, stage.at[(y + (1, 3)[e]) % N, core], y2.at[part, e], ring(e))
+
+    def dp_reduce1(part):
+        swap(part).wait_recv()
+
+        @pl.loop(0, N)
+        def _(k):
+            @pl.loop(0, N)
+            def _(g):
+                add(stage.at[k, core, g], pair.at[part, k, g])
+
+        for e in range(2):
+            ring1(part, e).start()
+
+    def dp_reduce2(part):
+        for e in range(2):
+            ring1(part, e).wait_recv()
+
+            @pl.loop(0, 2)
+            def _(g):
+                add(stage.at[(y + (1, 3)[e]) % N, core, 2 * e + g], y1.at[part, e, g])
+
+            ring2(part, e).start()
+
+    def dp_reduce3(part):
+        for e in range(2):
+            ring2(part, e).wait_recv()
+
+        @pl.loop(0, N)
+        def _(g):
+            grad_out[g, :, pl.ds(part * PART, PART)] = (
+                stage[y, core, g].astype(F32) + y2[part, 0, g].astype(F32) + y2[part, 1, g].astype(F32)
+            )
+
+        swap(part).wait_send()
+        for e in range(2):
+            ring1(part, e).wait_send()
+            ring2(part, e).wait_send()
 
     def info_copy(k):
         return pltpu.make_async_remote_copy(
@@ -318,59 +416,20 @@
 
     phases = {
         "A": matmul, "R1": reduce1, "R2": reduce2, "R3": reduce3, "R5": reduce5, "R6": reduce6,
-        "G2": gather2, "G3": gather3, "G4": gather4, "D": data_grad, "W": weight_grad,
+        "G2": gather2, "G3": gather3, "G4": gather4, "DL": data_grad_left, "D": data_grad,
+        "W": weight_grad, "Y1": dp_reduce1, "Y2": dp_reduce2, "Y3": dp_reduce3,
     }
+    seen, turned, loaded = set(), set(), set()
     for name, c in STEPS:
         phases[name](c)
 
-    def gw(k, src, dst, dev):
-        return pltpu.make_async_remote_copy(
-            src_ref=src, dst_ref=dst, send_sem=gw_send.at[k], recv_sem=gw_recv.at[k],
-            device_id=dev, device_id_type=MESH,
-        )
-
-    sibling = {"dp": 2 * y + 1 - core}
-    ring = [{"dp": (d + 2) % DP}, {"dp": (d + DP - 2) % DP}]
-    swap = gw(0, s.at[0, :, 1 - core], pair, sibling)
-    swap.start()
-    swap.wait_recv()
-
-    @pl.loop(0, N)
-    def _(k):
-        @pl.loop(0, N)
-        def _(g):
-            add(s.at[0, k, core, g], pair.at[k, g])
-
-    step1 = [gw(1 + e, s.at[0, (y + 2) % N, core, (LOW, HIGH)[e]], y1.at[e], ring[e]) for e in range(2)]
-    step2 = [gw(3 + e, s.at[0, (y + (1, 3)[e]) % N, core], y2.at[e], ring[e]) for e in range(2)]
-    for e in range(2):
-        step1[e].start()
-    for e in range(2):
-        step1[e].wait_recv()
-
-        @pl.loop(0, 2)
-        def _(g):
-            add(s.at[0, (y + (1, 3)[e]) % N, core, 2 * e + g], y1.at[e, g])
-
-        step2[e].start()
-    for e in range(2):
-        step2[e].wait_recv()
-
-    @pl.loop(0, N)
-    def _(g):
-        grad_out[g] = s[0, y, core, g].astype(F32) + y2[0, g].astype(F32) + y2[1, g].astype(F32)
-
-    swap.wait_send()
-    for e in range(2):
-        step1[e].wait_send()
-        step2[e].wait_send()
     own_info.wait()
     for k in range(1, DP):
         info_copy(k).wait_send()
         info_landing(k).wait_recv()
+    for c in range(ALL_CH):
+        sent(c)
     for c in range(CH):
-        if c:
-            sent(c)
         own_slot(c).wait()
         for k in range(1, DP):
             slot_copy(c, k).wait_send()
@@ -418,46 +477,49 @@
     vmem = pl.BlockSpec(memory_space=pltpu.VMEM)
     smem = pl.BlockSpec(memory_space=pltpu.SMEM)
     hbm = pl.BlockSpec(memory_space=pl.ANY)
-    tile = (TILE, WIDTH)
+    tile = (TILE, PART)
+    row = (TILE, WIDTH)
     dma = pltpu.SemaphoreType.DMA
     got, got_info, grad = pl.pallas_call(
         main_kernel,
         out_shape=(
             jax.ShapeDtypeStruct((CH, DP, BLOCK, FEAT), BF),
             jax.ShapeDtypeStruct((DP, 8, 128), jnp.int32),
-            jax.ShapeDtypeStruct((N,) + tile, F32),
+            jax.ShapeDtypeStruct((N,) + row, F32),
         ),
         in_specs=[smem, smem, vmem, hbm, hbm, hbm],
         out_specs=(hbm, hbm, vmem),
         scratch_shapes=[
             pltpu.VMEM((8, 128), jnp.int32),
             pltpu.VMEM((CH, N, BLOCK, FEAT), BF),
-            pltpu.VMEM((FEAT, ROWS), BF),
+            pltpu.VMEM((CH, FEAT, ROWS), BF),
             pltpu.VMEM((FEAT, WIDTH), BF),
-            pltpu.VMEM((CH, N, 2, N) + tile, BF),
-            pltpu.VMEM((CH, 2, 2, 2) + tile, BF),
-            pltpu.VMEM((CH, 2, 2, N) + tile, BF),
-            pltpu.VMEM((CH, 2, 2, TILE, HALF), BF),
-            pltpu.VMEM((CH, 2, 2) + tile, BF),
-            pltpu.VMEM((CH, 2, 2) + tile, BF),
-            pltpu.VMEM((CH, 2) + tile, BF),
+            pltpu.VMEM((ALL_CH, N, 2, N) + tile, BF),
+            pltpu.VMEM((ALL_CH, 2, 2, 2) + tile, BF),
+            pltpu.VMEM((ALL_CH, 2, 2, N) + tile, BF),
+            pltpu.VMEM((ALL_CH, 2, 2, TILE, HALF), BF),
+            pltpu.VMEM((ALL_CH, 2, 2) + tile, BF),
+            pltpu.VMEM((ALL_CH, 2, 2) + tile, BF),
+            pltpu.VMEM((ALL_CH, 2) + tile, BF),
             pltpu.VMEM((FEAT, WIDTH), F32),
+            pltpu.VMEM((ROWS, FEAT), F32),
             pltpu.VMEM((N, BLOCK, FEAT), BF),
             pltpu.VMEM((CH, DP, BLOCK, FEAT), BF),
-            pltpu.VMEM((N, N) + tile, BF),
-            pltpu.VMEM((2, 2) + tile, BF),
-            pltpu.VMEM((2, N) + tile, BF),
-            dma((CH + 1,)),
-            dma((CH, 2)),
-            dma((CH, 32)),
-            dma((CH, 32)),
+            pltpu.VMEM((N, 2, N) + tile, BF),
+            pltpu.VMEM((PARTS, N, N) + tile, BF),
+            pltpu.VMEM((PARTS, 2, 2) + tile, BF),
+            pltpu.VMEM((PARTS, 2, N) + tile, BF),
+            dma((CH + PARTS,)),
+            dma((ALL_CH, 2)),
+            dma((ALL_CH, 32)),
+            dma((ALL_CH, 32)),
             dma((CH, DP)),
             dma((CH, DP)),
             dma((CH,)),
             dma((DP,)),
             dma((DP,)),
-            dma((5,)),
-            dma((5,)),
+            dma((PARTS, 5)),
+            dma((PARTS, 5)),
         ],
         compiler_params=pltpu.CompilerParams(
             collective_id=0, has_side_effects=True, vmem_limit_bytes=67_000_000
@@ -475,7 +537,7 @@
         place_kernel,
         out_shape=(
             jax.ShapeDtypeStruct((CH * DP, BLOCK, FEAT), BF),
-            jax.ShapeDtypeStruct((N,) + tile, F32),
+            jax.ShapeDtypeStruct((N,) + row, F32),
         ),
         in_specs=[smem, hbm, hbm, hbm],
         out_specs=(hbm, hbm),
@@ -483,7 +545,7 @@
             pltpu.SMEM((DP, 8, 128), jnp.int32),
             pltpu.VMEM((CH, DP, BLOCK, FEAT), BF),
             pltpu.VMEM((BLOCK, FEAT), BF),
-            pltpu.VMEM((N,) + tile, F32),
+            pltpu.VMEM((N,) + row, F32),
             pltpu.SMEM((CH * DP,), jnp.int32),
             dma,
             dma,

time: 202 us -> 203 us (level); the launches traced: 201 us -> 200 us
  no operation moved by 1% of the time
where the time goes in v3:
time: 203 us; the launch traced here: 200 us
  Pallas kernels  200 us (99%)
    pallas_call x1, Pallas kernels, shards(): pl.pallas_call(main_kernel, out_shape=(jax.ShapeDtypeStruct((CH, DP, BLOC...  195 us
    pallas_call x1, Pallas kernels, shards(): pl.pallas_call(place_kernel, out_shape=(jax.ShapeDtypeStruct((CH * DP, BL...  4.76 us

profile of v3, /device:TPU:1, one launch (start us, length us, event | category | flops | bytes accessed | tf_op | source)
XLA Modules:
  0.0 200.2 jit_solution(14409669872218078786)
XLA Ops:
  0.6 194.8 %fused_backward.1 = (bf16[4,8,128,512]{3,2,1,0:T(8,128)(2,1)}, s32[8,8,128]{2,1,0:T(8,128)}, f32[4,16,3584]{2,1,0:T(8,128)}) custom-call(s32[16]{0:T(128)} %owner.1, s32[16]{0:T(128)} %offset.1, f32[3584]{0:T(1024)} %bias.1, bf16[4,4,128,512]{3,2,1,0:T(8,128)(2,1)} %bitcast.6, bf16[512,3584]{1,0:T(8,128)(2,1)} %w_hbm.1, bf16[4,4,2,4,16,3584]{5,4,3,2,1,0:T(8,128)(2,1)} %bitcast.5), custom_call_target="tpu_custom_call" | custom-call | tf_op jit(solution)/shard_map/fused_backward/pallas_call | solution.py:483
  195.5 4.8 %place_blocks.1 = (bf16[32,128,512]{2,1,0:T(8,128)(2,1)}, f32[4,16,3584]{2,1,0:T(8,128)}) custom-call(s32[1]{0:T(128)} %bitcast.me, s32[8,8,128]{2,1,0:T(8,128)} %get-tuple-element.7.info, bf16[4,8,128,512]{3,2,1,0:T(8,128)(2,1)} %get-tuple-element.8.got, f32[4,16,3584]{2,1,0:T(8,128)} %get-tuple-element.9.grad), custom_call_target="tpu_custom_call" | custom-call | tf_op jit(solution)/shard_map/place_blocks/pallas_call | solution.py:536

commit v4 on v3

--- a/solution.py
+++ b/solution.py
@@ -20,20 +20,21 @@
 HALF = PART // 2
 COL = 256
 ROWS = N * BLOCK
+FIRST, REST = (4, 2, 6), (3, 5, 7, 1, 0)
 MESH = pl.DeviceIdType.MESH
 BF = jnp.bfloat16
 F32 = jnp.float32
 STEPS = (
-    ("A", 1), ("R1", 1), ("A", 0), ("R1", 0), ("A", 3), ("R1", 3), ("A", 5), ("R1", 5), ("R2", 0), ("A", 6),
-    ("R2", 3), ("R3", 0), ("R2", 1), ("A", 2), ("A", 4), ("R5", 0), ("R1", 2), ("R1", 6), ("R3", 3), ("R2", 5),
-    ("R3", 1), ("R5", 3), ("R6", 0), ("R1", 4), ("R2", 2), ("R5", 1), ("R2", 4), ("A", 7), ("R3", 2), ("R6", 3),
-    ("R2", 6), ("G2", 3), ("R3", 4), ("R5", 2), ("R6", 1), ("G2", 0), ("G3", 3), ("G2", 1), ("G3", 0),
-    ("R5", 4), ("R6", 2), ("G4", 0), ("G3", 1), ("R6", 4), ("R3", 6), ("G2", 2), ("R3", 5), ("G4", 3),
-    ("G2", 4), ("R5", 6), ("R5", 5), ("R1", 7), ("G3", 2), ("R6", 5), ("W", 0), ("DL", 3), ("G4", 1), ("W", 3),
-    ("G4", 2), ("G3", 4), ("W", 1), ("G2", 5), ("R2", 7), ("W", 2), ("Y1", 0), ("G4", 4), ("R6", 6), ("R3", 7),
-    ("G3", 5), ("Y2", 0), ("D", 0), ("R5", 7), ("G2", 6), ("G4", 5), ("R6", 7), ("G3", 6), ("D", 1), ("Y3", 0),
-    ("G2", 7), ("G4", 6), ("W", 5), ("G3", 7), ("D", 2), ("G4", 7), ("W", 6), ("W", 4), ("W", 7), ("D", 3),
-    ("Y1", 1), ("Y2", 1), ("Y3", 1),
+    ("A", 1), ("R1", 1), ("A", 5), ("R1", 5), ("A", 4), ("R1", 4), ("R2", 1), ("A", 7), ("A", 6), ("A", 3),
+    ("R2", 4), ("R3", 1), ("R1", 7), ("A", 0), ("R1", 0), ("R1", 3), ("A", 2), ("R2", 5), ("R2", 3), ("R5", 1),
+    ("R3", 4), ("R3", 5), ("R1", 2), ("R1", 6), ("R6", 1), ("R2", 2), ("R5", 5), ("R2", 7), ("R3", 2),
+    ("R2", 0), ("R5", 2), ("R6", 5), ("R5", 4), ("G2", 1), ("R3", 0), ("R3", 3), ("G2", 5), ("R2", 6),
+    ("R5", 0), ("R6", 4), ("R5", 3), ("R6", 2), ("G3", 1), ("G2", 4), ("G3", 5), ("R6", 0), ("R3", 6),
+    ("G4", 1), ("R5", 6), ("G2", 0), ("G4", 5), ("G2", 2), ("G3", 4), ("G3", 0), ("R6", 3), ("D", 1), ("E", 1),
+    ("W", 5), ("G4", 4), ("G2", 3), ("R6", 6), ("G4", 0), ("W", 1), ("G3", 2), ("G3", 3), ("R3", 7), ("G4", 2),
+    ("G2", 6), ("D", 0), ("E", 0), ("G4", 3), ("W", 0), ("R5", 7), ("W", 2), ("G3", 6), ("W", 3), ("R6", 7),
+    ("Y1", 0), ("G4", 6), ("G2", 7), ("Y2", 0), ("G3", 7), ("D", 2), ("DL", 3), ("G4", 7), ("E", 2), ("W", 4),
+    ("W", 6), ("D", 3), ("Y3", 0), ("W", 7), ("Y1", 1), ("E", 3), ("Y2", 1), ("Y3", 1),
 )
 
 
@@ -94,7 +95,6 @@
             pl.semaphore_signal(barrier, inc=1, device_id=hop(axis, delta), device_id_type=MESH)
     for k in range(1, DP):
         pl.semaphore_signal(barrier, inc=1, device_id=peer(k), device_id_type=MESH)
-    pl.semaphore_wait(barrier, 4 + DP - 1)
 
     def rows(ref, h, f, g):
         return ref.at[f, 0, g] if h == 0 else ref.at[g, 1, f]
@@ -307,7 +307,10 @@
             out = (out + grad_part(c + CH, n)).astype(BF)
             gin[:, :, feature_tile(n)] = out.reshape(N, BLOCK, FEAT // 2)
 
-        for k in range(DP):
+        send_slots(c, FIRST)
+
+    def send_slots(c, which):
+        for k in which:
             target = (d + k) % DP
             pick = jnp.int32(0)
             for b in range(1, N):
@@ -317,6 +320,9 @@
                 slot_copy(c, k).start()
             else:
                 own_slot(c).start()
+
+    def data_send(c):
+        send_slots(c, REST)
 
     def weight_grad(c):
         landed(c)
@@ -410,17 +416,20 @@
         )
 
     own_info = pltpu.make_async_copy(info, got_info.at[d], info_send.at[0])
+
+    phases = {
+        "A": matmul, "R1": reduce1, "R2": reduce2, "R3": reduce3, "R5": reduce5, "R6": reduce6,
+        "G2": gather2, "G3": gather3, "G4": gather4, "DL": data_grad_left, "D": data_grad, "E": data_send,
+        "W": weight_grad, "Y1": dp_reduce1, "Y2": dp_reduce2, "Y3": dp_reduce3,
+    }
+    seen, turned, loaded = set(), set(), set()
+    phases[STEPS[0][0]](STEPS[0][1])
+    pl.semaphore_wait(barrier, 4 + DP - 1)
+    phases[STEPS[1][0]](STEPS[1][1])
     own_info.start()
     for k in range(1, DP):
         info_copy(k).start()
-
-    phases = {
-        "A": matmul, "R1": reduce1, "R2": reduce2, "R3": reduce3, "R5": reduce5, "R6": reduce6,
-        "G2": gather2, "G3": gather3, "G4": gather4, "DL": data_grad_left, "D": data_grad,
-        "W": weight_grad, "Y1": dp_reduce1, "Y2": dp_reduce2, "Y3": dp_reduce3,
-    }
-    seen, turned, loaded = set(), set(), set()
-    for name, c in STEPS:
+    for name, c in STEPS[2:]:
         phases[name](c)
 
     own_info.wait()
@@ -439,8 +448,9 @@
 def place_kernel(me, info, got, grad, out, grad_out, table, held, zeros, passed, flag, info_sem, in_sem, grad_sem, out_sem):
     fetch = pltpu.make_async_copy(info, table, info_sem)
     fetch.start()
-    load = pltpu.make_async_copy(got, held, in_sem)
-    load.start()
+    loads = [pltpu.make_async_copy(got.at[c], held.at[c], in_sem.at[c]) for c in range(CH)]
+    for load in loads:
+        load.start()
     take = pltpu.make_async_copy(grad, passed, grad_sem)
     take.start()
     zeros[...] = jnp.zeros_like(zeros)
@@ -448,14 +458,12 @@
     for j in range(count):
         flag[j] = 0
     fetch.wait()
-    load.wait()
-    take.wait()
     give = pltpu.make_async_copy(passed, grad_out, grad_sem)
-    give.start()
     mine = me[0]
-    for source in range(DP):
-        for b in range(N):
-            for c in range(CH):
+    for c in range(CH):
+        loads[c].wait()
+        for source in range(DP):
+            for b in range(N):
 
                 @pl.when(table[source, 0, b * CH + c] == mine)
                 def _():
@@ -463,6 +471,8 @@
                     flag[row] = 1
                     pltpu.make_async_copy(held.at[c, source], out.at[row], out_sem).start()
 
+    take.wait()
+    give.start()
     for j in range(count):
 
         @pl.when(flag[j] == 0)
@@ -548,7 +558,7 @@
             pltpu.VMEM((N,) + row, F32),
             pltpu.SMEM((CH * DP,), jnp.int32),
             dma,
-            dma,
+            dma((CH,)),
             dma,
             dma,
         ],

time: 203 us -> 201 us (level); the launches traced: 200 us -> 201 us
  no operation moved by 1% of the time
where the time goes in v4:
time: 201 us
  Pallas kernels  200 us (100%)
    pallas_call x1, Pallas kernels, shards(): pl.pallas_call(main_kernel, out_shape=(jax.ShapeDtypeStruct((CH, DP, BLOC...  196 us

profile of v4, /device:TPU:1, one launch (start us, length us, event | category | flops | bytes accessed | tf_op | source)
XLA Modules:
  0.0 200.6 jit_solution(2049905623557415752)
XLA Ops:
  0.6 196.1 %fused_backward.1 = (bf16[4,8,128,512]{3,2,1,0:T(8,128)(2,1)}, s32[8,8,128]{2,1,0:T(8,128)}, f32[4,16,3584]{2,1,0:T(8,128)}) custom-call(s32[16]{0:T(128)} %owner.1, s32[16]{0:T(128)} %offset.1, f32[3584]{0:T(1024)} %bias.1, bf16[4,4,128,512]{3,2,1,0:T(8,128)(2,1)} %bitcast.6, bf16[512,3584]{1,0:T(8,128)(2,1)} %w_hbm.1, bf16[4,4,2,4,16,3584]{5,4,3,2,1,0:T(8,128)(2,1)} %bitcast.5), custom_call_target="tpu_custom_call" | custom-call | tf_op jit(solution)/shard_map/fused_backward/pallas_call | solution.py:493
  196.7 3.9 %place_blocks.1 = (bf16[32,128,512]{2,1,0:T(8,128)(2,1)}, f32[4,16,3584]{2,1,0:T(8,128)}) custom-call(s32[1]{0:T(128)} %bitcast.me, s32[8,8,128]{2,1,0:T(8,128)} %get-tuple-element.7.info, bf16[4,8,128,512]{3,2,1,0:T(8,128)(2,1)} %get-tuple-element.8.got, f32[4,16,3584]{2,1,0:T(8,128)} %get-tuple-element.9.grad), custom_call_target="tpu_custom_call" | custom-call | tf_op jit(solution)/shard_map/place_blocks/pallas_call | solution.py:546
